TPU v7x, 512 devices: a whole 4x8x8 slice. The times are simulated.
512 devices in a mesh: dp: 16 (over y, z_lo), fsdp: 32 (over x, z_hi, core).
Axes of the slice: x: 4, y: 8, z: 8 (z_hi: 4, z_lo: 2; z = z_hi * 2 + z_lo), core: 2. Of those that a mesh axis runs over, the one named last changes fastest.
Arguments:
- signal: bfloat16 [131072, 1024], P(('dp', 'fsdp')), may hold values from -6 to 6
- grad_gated: bfloat16 [131072, 512], P(('dp', 'fsdp')), may hold values from -24 to 24
- conv_weight: bfloat16 [1024, 3072], P('fsdp'), may hold values from -0.109375 to 0.109375
- source_seg: int32 [512, 32], P(('dp', 'fsdp')), may hold values from -1 to 1023, as said below
Outputs:
- gated_out: bfloat16 [131072, 512], P(('dp', 'fsdp'))
- grad_in: bfloat16 [131072, 1024], P(('dp', 'fsdp'))
- grad_weight: float32 [1024, 3072], P('fsdp')
Inputs may be any that keep to these rules, and one draw needn't show every extreme that they name: `source_seg`: -1 where a stream begins. The preceding segment holds the same position on its device as g on its own, no two segments of one device take their left context from the same device, and every segment precedes at most one segment.
All inputs are finite; a program needn't handle non-finite values.
Results may differ from a plain program's by a relative error of at most 0.0049.
Values may be sent and summed in bfloat16 or wider, within the bound.
A program may use at most 64 MiB of HBM per device.

v0:
```python
import math
import jax
import jax.numpy as jnp
from jax import lax
from jax.sharding import PartitionSpec as P

C = 1024
H = 512
DILATION_SIZE = 4


def tap_starts(context_row_block):
    return [context_row_block - (2 - selected_index) * DILATION_SIZE for selected_index in range(3)]


def per_device(signal, grad_gated, conv_weight, source_seg):
    peer_count = lax.axis_size("fsdp")
    seg_count = source_seg.shape[1]
    row_count = signal.shape[0]
    seg_rows = row_count // seg_count
    context_row_block = 2 * DILATION_SIZE
    starts = tap_starts(context_row_block)
    segments = signal.reshape(seg_count, seg_rows, C)
    sources = source_seg[0]
    source_dev = jnp.where(sources >= 0, sources // seg_count, -1)
    peers = jnp.arange(peer_count, dtype=jnp.int32)
    request_mask = (source_dev[None, :] == peers[:, None]).astype(jnp.int32)
    asked = lax.all_to_all(request_mask, "fsdp", split_axis=0, concat_axis=0, tiled=True)
    send_table = asked.astype(jnp.bfloat16)
    recv_table = (source_dev[:, None] == peers[None, :]).astype(jnp.bfloat16)
    outgoing = jnp.einsum(
        "ns,slc->nlc", send_table, segments, preferred_element_type=jnp.float32
    ).astype(jnp.bfloat16)
    incoming = lax.all_to_all(outgoing, "fsdp", split_axis=0, concat_axis=0, tiled=True)
    carries = jnp.einsum(
        "sn,nlc->slc", recv_table, incoming, preferred_element_type=jnp.float32
    ).astype(jnp.bfloat16)
    extended = jnp.concatenate([carries, segments], axis=1)
    full_weight = lax.all_gather(conv_weight, "fsdp", axis=0, tiled=True)
    contract_final_axis = (((1,), (1,)), ((), ()))
    contract_first = (((0,), (0,)), ((), ()))
    windows = [extended[:, start : start + seg_rows, :].reshape(row_count, C) for start in starts]
    preact = sum(
        (
            lax.dot_general(
                windows[selected_index],
                full_weight[:, selected_index * C : (selected_index + 1) * C],
                contract_final_axis,
                preferred_element_type=jnp.float32,
            )
            for selected_index in range(3)
        )
    )
    filter_act = jnp.tanh(preact[:, :H])
    gate_act = jax.nn.sigmoid(preact[:, H:])
    gated_out = (filter_act * gate_act).astype(jnp.bfloat16)
    upstream_wide = grad_gated.astype(jnp.float32)
    grad_pre = jnp.concatenate(
        [
            upstream_wide * gate_act * (1.0 - filter_act * filter_act),
            upstream_wide * filter_act * gate_act * (1.0 - gate_act),
        ],
        axis=1,
    ).astype(jnp.bfloat16)
    partial_value = jnp.concatenate(
        [
            lax.dot_general(
                grad_pre,
                windows[selected_index],
                contract_first,
                preferred_element_type=jnp.float32,
            ).astype(jnp.bfloat16)
            for selected_index in range(3)
        ],
        axis=1,
    )
    arrived = lax.all_to_all(partial_value, "fsdp", split_axis=0, concat_axis=0, tiled=True)
    shard_sum = jnp.sum(arrived.reshape(peer_count, -1, 3 * C), axis=0, dtype=jnp.float32)
    group_total = lax.psum(shard_sum, "dp")
    total_token_count = row_count * peer_count * lax.axis_size("dp")
    grad_weight = group_total * (1.0 / math.sqrt(total_token_count))
    back_proj = jnp.dot(grad_pre, full_weight, preferred_element_type=jnp.float32)
    back_proj = back_proj.reshape(seg_count, seg_rows, 3 * C)
    grad_ext = jnp.zeros((seg_count, context_row_block + seg_rows, C), jnp.float32)
    for selected_index, start in enumerate(starts):
        grad_ext = grad_ext.at[:, start : start + seg_rows, :].add(
            back_proj[:, :, selected_index * C : (selected_index + 1) * C]
        )
    outgoing_grad = jnp.einsum(
        "sn,slc->nlc",
        recv_table.astype(jnp.float32),
        grad_ext[:, :context_row_block, :],
        precision=lax.Precision.HIGHEST,
    )
    incoming_grad = lax.all_to_all(outgoing_grad, "fsdp", split_axis=0, concat_axis=0, tiled=True)
    tail_grad = jnp.einsum(
        "ns,nlc->slc",
        send_table.astype(jnp.float32),
        incoming_grad,
        precision=lax.Precision.HIGHEST,
    )
    grad_in = (
        grad_ext[:, context_row_block:, :].at[:, seg_rows - context_row_block :, :].add(tail_grad)
    )
    grad_in = grad_in.reshape(row_count, C).astype(jnp.bfloat16)
    return (gated_out, grad_in, grad_weight)


def solution(mesh):
    placed = (
        P(("dp", "fsdp"), None),
        P(("dp", "fsdp"), None),
        P("fsdp", None),
        P(("dp", "fsdp"), None),
    )
    return jax.shard_map(
        per_device,
        mesh=mesh,
        in_specs=placed,
        out_specs=(P(("dp", "fsdp"), None), P(("dp", "fsdp"), None), P("fsdp", None)),
        check_vma=False,
    )
```

profile of v0, /device:TPU:2, one launch (start us, length us, event | category | flops | bytes accessed | tf_op | source)
XLA Modules:
  0.0 440.9 jit_solution(733692016285793341)
XLA Ops:
  7.2 0.0 copy-start.2
  7.2 0.0 copy-start
  7.2 0.0 all-gather.2.cloned.1.call-start
  7.2 0.7 all-gather.2.cloned.1.call-update
  7.9 0.7 fusion.43
  8.6 21.8 %all_to_all.25 = s32[32,1,32]{2,1,0:T(1,128)S(1)} all-to-all(s32[32,1,32]{2,1,0:T(1,128)S(1)} %compare_convert_fusion), channel_id=1, replica_groups=mesh['dp'=16,'fsdp'=32] {'fsdp'}, dimensions={0} | all-to-all | bytes 8192 | tf_op jit(solution)/shard_map/all_to_all | solution.py:28
  30.4 1.8 convolution_convert_fusion.4
  32.3 1.1 copy.20
  33.4 5.0 %all-to-all-start.1 = ((bf16[32,8,1024]{2,1,0:T(8,128)(2,1)}), bf16[32,8,1024]{2,1,0:T(8,128)(2,1)S(1)}, u32[]{:S(2)}, u32[]{:S(2)}) async-start(bf16[32,8,1024]{2,1,0:T(8,128)(2,1)} %copy.20), calls=%async_computation.1 | async-start | bytes 1048576 | tf_op jit(solution)/shard_map/all_to_all | solution.py:34
  38.4 1.3 copy.19
  39.7 0.0 copy-done.2
  39.8 17.5 %all-to-all-done.1 = bf16[32,8,1024]{2,1,0:T(8,128)(2,1)S(1)} async-done(((bf16[32,8,1024]{2,1,0:T(8,128)(2,1)}), bf16[32,8,1024]{2,1,0:T(8,128)(2,1)S(1)}, u32[]{:S(2)}, u32[]{:S(2)}) %all-to-all-start.1) | async-done | bytes 524320 | tf_op jit(solution)/shard_map/all_to_all | solution.py:34
  57.3 0.8 convolution_convert_fusion.3
  58.1 39.0 %all-gather.2.cloned.1.call-done = bf16[1024,3072]{1,0:T(8,128)(2,1)} async-done(((bf16[32,3072]{1,0:T(8,128)(2,1)}), bf16[1024,3072]{1,0:T(8,128)(2,1)}) %all-gather.2.cloned.1.call-update) | async-done | bytes 6291472 | tf_op jit(solution)/shard_map/all_gather | solution.py:39
  97.1 0.0 copy-done
  97.1 2.3 fusion
  99.4 0.0 copy-start.1
  99.4 2.5 fusion.2
  101.9 2.5 fusion.9
  104.4 0.0 copy-done.1
  104.4 1.0 fusion.18
  105.4 0.8 convolution_convert_fusion.2
  106.3 0.8 convolution_convert_fusion.1
  107.1 0.8 convolution_convert_fusion
  107.9 13.4 %pad_maximum_fusion = bf16[1024,3072]{0,1:T(8,128)(2,1)} fusion(bf16[1024,1024]{0,1:T(8,128)(2,1)S(1)} %convolution_convert_fusion, bf16[1024,1024]{0,1:T(8,128)(2,1)S(1)} %convolution_convert_fusion.1, bf16[1024,1024]{0,1:T(8,128)(2,1)S(1)} %convolution_convert_fusion.2), kind=kLoop, calls=%fused_computation.1 | loop fusion | flops 18874368 | bytes 12582912 | tf_op jit(solution)/shard_map/concatenate | solution.py:65
  121.3 8.6 %copy.33 = bf16[1024,3072]{1,0:T(8,128)(2,1)} copy(bf16[1024,3072]{0,1:T(8,128)(2,1)} %pad_maximum_fusion) | data formatting | bytes 12582912 | tf_op jit(solution)/shard_map/concatenate | solution.py:65
  129.9 6.8 %all-to-all-start.3 = ((bf16[32,32,3072]{2,1,0:T(8,128)(2,1)}), bf16[32,32,3072]{2,1,0:T(8,128)(2,1)}, u32[]{:S(2)}, u32[]{:S(2)}) async-start(bf16[32,32,3072]{2,1,0:T(8,128)(2,1)} %bitcast.44), calls=%async_computation.3 | async-start | bytes 12582912 | tf_op jit(solution)/shard_map/all_to_all | solution.py:77
  136.7 4.6 %convolution_bitcast_fusion = f32[32,8,3072]{2,1,0:T(8,128)S(1)} fusion(bf16[1024,3072]{1,0:T(8,128)(2,1)} %all-gather.2.cloned.1.call-done, bf16[256,512]{1,0:T(8,128)(2,1)S(1)} %get-tuple-element.63, bf16[256,512]{1,0:T(8,128)(2,1)S(1)} %get-tuple-element.62), kind=kOutput, calls=%fused_computation.2 | convolution fusion | flops 1611661312 | bytes 9961472 | tf_op jit(solution)/shard_map/dot_general | solution.py:82
  141.3 1.4 fusion.45
  142.7 0.6 copy.38
  143.3 0.2 scatter-add.6
  143.6 1.0 fusion.15
  144.5 0.6 fusion.13
  145.2 1.6 copy.29
  146.7 130.2 %all-to-all-done.3 = bf16[32,32,3072]{2,1,0:T(8,128)(2,1)} async-done(((bf16[32,32,3072]{2,1,0:T(8,128)(2,1)}), bf16[32,32,3072]{2,1,0:T(8,128)(2,1)}, u32[]{:S(2)}, u32[]{:S(2)}) %all-to-all-start.3) | async-done | bytes 6291488 | tf_op jit(solution)/shard_map/all_to_all | solution.py:77
  277.0 8.6 %all-to-all-start.2 = ((f32[32,8,1024]{2,1,0:T(8,128)}), f32[32,8,1024]{2,1,0:T(8,128)S(1)}, u32[]{:S(2)}, u32[]{:S(2)}) async-start(f32[32,8,1024]{2,1,0:T(8,128)} %copy.29), calls=%async_computation.2 | async-start | bytes 2097152 | tf_op jit(solution)/shard_map/all_to_all | solution.py:95
  285.6 0.0 all-reduce.3.cloned.1.call-start
  285.6 4.8 %convert_reduce_fusion = f32[32,3072]{1,0:T(8,128)} fusion(bf16[32,32,3072]{2,1,0:T(8,128)(2,1)} %all-to-all-done.3), kind=kLoop, calls=%fused_computation | loop fusion | flops 6193152 | bytes 6684672 | tf_op jit(solution)/shard_map/reduce_sum | solution.py:78
  290.4 0.0 all-reduce.3.cloned.1.call-update
  290.5 20.6 %all-to-all-done.2 = f32[32,8,1024]{2,1,0:T(8,128)S(1)} async-done(((f32[32,8,1024]{2,1,0:T(8,128)}), f32[32,8,1024]{2,1,0:T(8,128)S(1)}, u32[]{:S(2)}, u32[]{:S(2)}) %all-to-all-start.2) | async-done | bytes 1048608 | tf_op jit(solution)/shard_map/all_to_all | solution.py:95
  311.1 3.0 fusion.12
  314.1 1.1 copy.68
  315.2 117.1 %all-reduce.3.cloned.1.call-done = f32[32,3072]{1,0:T(8,128)} async-done(((f32[32,3072]{1,0:T(8,128)}), f32[32,3072]{1,0:T(8,128)}) %all-reduce.3.cloned.1.call-update) | async-done | bytes 393232 | tf_op jit(solution)/shard_map/psum | solution.py:79
  432.3 1.8 broadcast_multiply_fusion
  (3 shorter events, 0.1 us)
Async XLA Ops:
  7.2 32.6 %copy-start.2 = (s32[1,32]{1,0:T(1,128)S(1)}, s32[1,32]{1,0:T(1,128)}, u32[]{:S(2)}) copy-start(s32[1,32]{1,0:T(1,128)} %param.17) | copy-start | bytes 388
  7.2 89.9 %copy-start = (bf16[256,1024]{1,0:T(8,128)(2,1)S(1)}, bf16[256,1024]{1,0:T(8,128)(2,1)}, u32[]{:S(2)}) copy-start(bf16[256,1024]{1,0:T(8,128)(2,1)} %param.14) | copy-start | bytes 1572868
  7.2 89.9 %all-gather.2.cloned.1.call-start = ((), (), s32[]{:S(2)}) async-start(), calls=%async_computation.4 | async-start | bytes 6488064 | tf_op jit(solution)/shard_map/all_gather | solution.py:39
  33.4 23.9 %all-to-all-start.1 = ((bf16[32,8,1024]{2,1,0:T(8,128)(2,1)}), bf16[32,8,1024]{2,1,0:T(8,128)(2,1)S(1)}, u32[]{:S(2)}, u32[]{:S(2)}) async-start(bf16[32,8,1024]{2,1,0:T(8,128)(2,1)} %copy.20), calls=%async_computation.1 | async-start | bytes 1048576 | tf_op jit(solution)/shard_map/all_to_all | solution.py:34
  99.4 5.0 %copy-start.1 = (bf16[256,512]{1,0:T(8,128)(2,1)S(1)}, bf16[256,512]{1,0:T(8,128)(2,1)}, u32[]{:S(2)}) copy-start(bf16[256,512]{1,0:T(8,128)(2,1)} %param.15) | copy-start | bytes 786436
  129.9 147.1 %all-to-all-start.3 = ((bf16[32,32,3072]{2,1,0:T(8,128)(2,1)}), bf16[32,32,3072]{2,1,0:T(8,128)(2,1)}, u32[]{:S(2)}, u32[]{:S(2)}) async-start(bf16[32,32,3072]{2,1,0:T(8,128)(2,1)} %bitcast.44), calls=%async_computation.3 | async-start | bytes 12582912 | tf_op jit(solution)/shard_map/all_to_all | solution.py:77
  277.0 34.1 %all-to-all-start.2 = ((f32[32,8,1024]{2,1,0:T(8,128)}), f32[32,8,1024]{2,1,0:T(8,128)S(1)}, u32[]{:S(2)}, u32[]{:S(2)}) async-start(f32[32,8,1024]{2,1,0:T(8,128)} %copy.29), calls=%async_computation.2 | async-start | bytes 2097152 | tf_op jit(solution)/shard_map/all_to_all | solution.py:95
  285.6 146.7 %all-reduce.3.cloned.1.call-start = ((), (), s32[]{:S(2)}) async-start(), calls=%async_computation.5 | async-start | bytes 786432 | tf_op jit(solution)/shard_map/psum | solution.py:79
Sparse Core Ops, SparseCore 0:
  11.1 85.8 all-gather.1
  290.6 141.6 all-reduce.2
where the time goes:
time: 442 us; the launch traced here: 441 us
  waiting for transfers between devices  325 us (74%)
  other arithmetic  22.7 us (5%)
  blocking collectives  21.8 us (5%)
  starting transfers between devices  20.5 us (5%)
  matrix products  20.5 us (5%)
  local copies, waits for them, and re-layouts  16 us (4%)
  between operations  14.2 us (3%)
    all_to_all x1, waiting for transfers between devices, per_device(): lax.all_to_all(partial_value, 'fsdp', split_axis=0, concat_axis=0, tiled=...  130 us
    psum x1, waiting for transfers between devices, per_device(): group_total = lax.psum(shard_sum, 'dp')  117 us
    all_gather x1, waiting for transfers between devices, per_device(): full_weight = lax.all_gather(conv_weight, 'fsdp', axis=0, tiled=True)  39 us
    all_to_all x1, blocking collectives, per_device(): lax.all_to_all(request_mask, 'fsdp', split_axis=0, concat_axis=0, tiled=T...  21.8 us
    all_to_all x1, waiting for transfers between devices, per_device(): lax.all_to_all(outgoing_grad, 'fsdp', split_axis=0, concat_axis=0, tiled=...  20.6 us
    all_to_all x1, waiting for transfers between devices, per_device(): lax.all_to_all(outgoing, 'fsdp', split_axis=0, concat_axis=0, tiled=True)  17.5 us
    concatenate x1, other arithmetic, per_device(): jnp.concatenate([lax.dot_general(grad_pre, windows[selected_index], contr...  13.4 us
  transfers between devices with their start and end apart: 5, of which 5 were waited for; matrix products, arithmetic and copies ran while one was open for 6% of the time, Pallas kernels for 0%

commit v1 on v0

--- a/solution.py
+++ b/solution.py
@@ -76,7 +76,7 @@
     )
     arrived = lax.all_to_all(partial_value, "fsdp", split_axis=0, concat_axis=0, tiled=True)
     shard_sum = jnp.sum(arrived.reshape(peer_count, -1, 3 * C), axis=0, dtype=jnp.float32)
-    group_total = lax.psum(shard_sum, "dp")
+    group_total = jnp.sum(lax.all_gather(shard_sum, "dp"), axis=0)
     total_token_count = row_count * peer_count * lax.axis_size("dp")
     grad_weight = group_total * (1.0 / math.sqrt(total_token_count))
     back_proj = jnp.dot(grad_pre, full_weight, preferred_element_type=jnp.float32)

time: 442 us -> 456 us (1.032)
  the two profiles are of different devices: /device:TPU:2 before, /device:TPU:27 now
where the time goes in v1:
time: 456 us; the launch traced here: 455 us
  blocking collectives  227 us (50%)
  waiting for transfers between devices  153 us (34%)
  other arithmetic  22 us (5%)
  matrix products  19.3 us (4%)
  between operations  14.2 us (3%)
  local copies, waits for them, and re-layouts  14 us (3%)
  starting transfers between devices  5.29 us (1%)
    all_to_all x1, blocking collectives, per_device(): lax.all_to_all(partial_value, 'fsdp', split_axis=0, concat_axis=0, tiled=...  148 us
    all_gather x1, waiting for transfers between devices, per_device(): group_total = jnp.sum(lax.all_gather(shard_sum, 'dp'), axis=0)  96.1 us
    all_to_all x1, blocking collectives, per_device(): lax.all_to_all(outgoing_grad, 'fsdp', split_axis=0, concat_axis=0, tiled=...  57.8 us
    all_gather x1, waiting for transfers between devices, per_device(): full_weight = lax.all_gather(conv_weight, 'fsdp', axis=0, tiled=True)  39.4 us
    all_to_all x1, blocking collectives, per_device(): lax.all_to_all(request_mask, 'fsdp', split_axis=0, concat_axis=0, tiled=T...  21.9 us
    all_to_all x1, waiting for transfers between devices, per_device(): lax.all_to_all(outgoing, 'fsdp', split_axis=0, concat_axis=0, tiled=True)  16.9 us
    concatenate x1, other arithmetic, per_device(): jnp.concatenate([lax.dot_general(grad_pre, windows[selected_index], contr...  13.4 us
  transfers between devices with their start and end apart: 3, of which 3 were waited for; matrix products, arithmetic and copies ran while one was open for 4% of the time, Pallas kernels for 0%

profile of v1, /device:TPU:27, one launch (start us, length us, event | category | flops | bytes accessed | tf_op | source)
XLA Modules:
  0.0 455.1 jit_solution(9515092726578908465)
XLA Ops:
  7.2 0.0 copy-start.2
  7.2 0.0 copy-start
  7.2 0.0 all-gather.4.cloned.1.call-start
  7.2 0.7 all-gather.4.cloned.1.call-update
  7.9 0.7 fusion.43
  8.6 21.9 %all_to_all.25 = s32[32,1,32]{2,1,0:T(1,128)S(1)} all-to-all(s32[32,1,32]{2,1,0:T(1,128)S(1)} %compare_convert_fusion), channel_id=1, replica_groups=mesh['dp'=16,'fsdp'=32] {'fsdp'}, dimensions={0} | all-to-all | bytes 8192 | tf_op jit(solution)/shard_map/all_to_all | solution.py:28
  30.6 1.8 convolution_convert_fusion.4
  32.4 1.1 copy.36
  33.5 5.2 %all-to-all-start.1 = ((bf16[32,8,1024]{2,1,0:T(8,128)(2,1)}), bf16[32,8,1024]{2,1,0:T(8,128)(2,1)S(1)}, u32[]{:S(2)}, u32[]{:S(2)}) async-start(bf16[32,8,1024]{2,1,0:T(8,128)(2,1)} %copy.36), calls=%async_computation.1 | async-start | bytes 1048576 | tf_op jit(solution)/shard_map/all_to_all | solution.py:34
  38.7 0.0 all-gather.6.cloned.1.call-start
  38.8 1.3 copy.35
  40.1 0.0 copy-done.2
  40.1 16.9 %all-to-all-done.1 = bf16[32,8,1024]{2,1,0:T(8,128)(2,1)S(1)} async-done(((bf16[32,8,1024]{2,1,0:T(8,128)(2,1)}), bf16[32,8,1024]{2,1,0:T(8,128)(2,1)S(1)}, u32[]{:S(2)}, u32[]{:S(2)}) %all-to-all-start.1) | async-done | bytes 524320 | tf_op jit(solution)/shard_map/all_to_all | solution.py:34
  57.1 0.8 convolution_convert_fusion.3
  57.9 39.4 %all-gather.4.cloned.1.call-done = bf16[1024,3072]{1,0:T(8,128)(2,1)} async-done(((bf16[32,3072]{1,0:T(8,128)(2,1)}), bf16[1024,3072]{1,0:T(8,128)(2,1)}) %all-gather.4.cloned.1.call-update) | async-done | bytes 6291472 | tf_op jit(solution)/shard_map/all_gather | solution.py:39
  97.2 0.0 copy-done
  97.2 2.3 fusion
  99.6 0.0 copy-start.1
  99.6 2.5 fusion.2
  102.1 2.5 fusion.9
  104.6 0.0 copy-done.1
  104.6 1.0 fusion.18
  105.6 0.8 convolution_convert_fusion.2
  106.4 0.8 convolution_convert_fusion.1
  107.3 0.8 convolution_convert_fusion
  108.1 13.4 %pad_maximum_fusion = bf16[1024,3072]{0,1:T(8,128)(2,1)} fusion(bf16[1024,1024]{0,1:T(8,128)(2,1)S(1)} %convolution_convert_fusion, bf16[1024,1024]{0,1:T(8,128)(2,1)S(1)} %convolution_convert_fusion.1, bf16[1024,1024]{0,1:T(8,128)(2,1)S(1)} %convolution_convert_fusion.2), kind=kLoop, calls=%fused_computation.1 | loop fusion | flops 18874368 | bytes 12582912 | tf_op jit(solution)/shard_map/concatenate | solution.py:65
  121.4 8.6 %copy.49 = bf16[1024,3072]{1,0:T(8,128)(2,1)} copy(bf16[1024,3072]{0,1:T(8,128)(2,1)} %pad_maximum_fusion) | data formatting | bytes 12582912 | tf_op jit(solution)/shard_map/concatenate | solution.py:65
  130.1 147.5 %all_to_all.26 = bf16[32,32,3072]{2,1,0:T(8,128)(2,1)S(1)} all-to-all(bf16[32,32,3072]{2,1,0:T(8,128)(2,1)} %bitcast.45), channel_id=1, replica_groups=mesh['dp'=16,'fsdp'=32] {'fsdp'}, dimensions={0} | all-to-all | bytes 12582912 | tf_op jit(solution)/shard_map/all_to_all | solution.py:77
  277.6 2.0 convert_reduce_fusion
  279.6 0.0 all-gather.6.cloned.1.call-update
  279.6 4.6 %convolution_bitcast_fusion = f32[32,8,3072]{2,1,0:T(8,128)S(1)} fusion(bf16[1024,3072]{1,0:T(8,128)(2,1)} %all-gather.4.cloned.1.call-done, bf16[256,512]{1,0:T(8,128)(2,1)S(1)} %get-tuple-element.63, bf16[256,512]{1,0:T(8,128)(2,1)S(1)} %get-tuple-element.62), kind=kOutput, calls=%fused_computation.2 | convolution fusion | flops 1611661312 | bytes 9961472 | tf_op jit(solution)/shard_map/dot_general | solution.py:82
  284.2 0.3 fusion.45
  284.5 0.6 copy.54
  285.1 0.2 scatter-add.6
  285.4 1.0 fusion.15
  286.3 0.6 fusion.13
  287.0 0.6 copy.45
  287.6 57.8 %all_to_all.27 = f32[32,8,1024]{2,1,0:T(8,128)S(1)} all-to-all(f32[32,8,1024]{2,1,0:T(8,128)S(1)} %copy.45), channel_id=1, replica_groups=mesh['dp'=16,'fsdp'=32] {'fsdp'}, dimensions={0} | all-to-all | bytes 2097152 | tf_op jit(solution)/shard_map/all_to_all | solution.py:95
  345.4 1.8 fusion.12
  347.2 1.1 copy.84
  348.3 96.1 %all-gather.6.cloned.1.call-done = f32[512,3072]{1,0:T(8,128)} async-done(((f32[32,3072]{1,0:T(8,128)}), f32[512,3072]{1,0:T(8,128)}) %all-gather.6.cloned.1.call-update) | async-done | bytes 6291472 | tf_op jit(solution)/shard_map/all_gather | solution.py:79
  444.4 3.1 reduce_sum.19
  447.5 0.8 broadcast_multiply_fusion
  (3 shorter events, 0.1 us)
Async XLA Ops:
  7.2 32.9 %copy-start.2 = (s32[1,32]{1,0:T(1,128)S(1)}, s32[1,32]{1,0:T(1,128)}, u32[]{:S(2)}) copy-start(s32[1,32]{1,0:T(1,128)} %param.17) | copy-start | bytes 388
  7.2 90.1 %copy-start = (bf16[256,1024]{1,0:T(8,128)(2,1)S(1)}, bf16[256,1024]{1,0:T(8,128)(2,1)}, u32[]{:S(2)}) copy-start(bf16[256,1024]{1,0:T(8,128)(2,1)} %param.14) | copy-start | bytes 1572868
  7.2 90.1 %all-gather.4.cloned.1.call-start = ((), (), s32[]{:S(2)}) async-start(), calls=%async_computation.4 | async-start | bytes 6488064 | tf_op jit(solution)/shard_map/all_gather | solution.py:39
  33.5 23.6 %all-to-all-start.1 = ((bf16[32,8,1024]{2,1,0:T(8,128)(2,1)}), bf16[32,8,1024]{2,1,0:T(8,128)(2,1)S(1)}, u32[]{:S(2)}, u32[]{:S(2)}) async-start(bf16[32,8,1024]{2,1,0:T(8,128)(2,1)} %copy.36), calls=%async_computation.1 | async-start | bytes 1048576 | tf_op jit(solution)/shard_map/all_to_all | solution.py:34
  38.7 405.7 %all-gather.6.cloned.1.call-start = ((), (), s32[]{:S(2)}) async-start(), calls=%async_computation.5 | async-start | bytes 6684672 | tf_op jit(solution)/shard_map/all_gather | solution.py:79
  99.6 5.0 %copy-start.1 = (bf16[256,512]{1,0:T(8,128)(2,1)S(1)}, bf16[256,512]{1,0:T(8,128)(2,1)}, u32[]{:S(2)}) copy-start(bf16[256,512]{1,0:T(8,128)(2,1)} %param.15) | copy-start | bytes 786436
Sparse Core Ops, SparseCore 0:
  11.1 86.0 all-gather.3
  279.7 164.6 all-gather.5
